TPU v7x, 32 devices: a whole 2x2x4 slice. The times are simulated.
32 devices in a mesh: group: 2 (over y), frame: 8 (over z, x), row: 2 (over core).
Axes of the slice: x: 2, y: 2, z: 4, core: 2. Of those that a mesh axis runs over, the one named last changes fastest.
Arguments:
- latents: bfloat16 [16, 8, 32, 1120], P(('group', 'frame'), 'row'), parts along dimension 0, may hold values from -24 to 24
- spatial_weights: bfloat16 [4, 10, 112, 112], replicated, may hold values from -0.5 to 0.5
- causal_weights: bfloat16 [4, 10, 112, 112], replicated, may hold values from -0.5 to 0.5
Outputs:
- updated_latents: bfloat16 [16, 8, 32, 1120], P(('group', 'frame'), None, None, 'row'), parts along dimension 0
There are 2 independent parts, one for each index of `group`. A program takes and returns all parts, laid end to end along the dimension named above; an argument that names none is the same for every part. Nothing has to cross between parts.
All inputs are finite; a program needn't handle non-finite values.
Results may differ from a plain program's by a relative error of at most 0.0047.
The roundings to bfloat16 on the way count: a program that leaves them out, or rounds other values in their place, can miss the bound.
Values may be sent and summed in bfloat16 or wider, within the bound.
No kernel may reach another device: no remote copies, remote signals or barrier semaphores. Data moves between devices by JAX's collectives and lax.ppermute only.
A program may use at most 64 MiB of HBM per device.

v0:
```python
import jax
import jax.numpy as jnp
from jax import lax
from jax.sharding import PartitionSpec as P


def prefix(x, axis, join, neutral):
    place = lax.axis_index(axis)
    gathered = lax.all_gather(x.astype(jnp.bfloat16), axis)
    state = jnp.zeros_like(x) + jnp.asarray(neutral, x.dtype)

    def one(turn, state):
        return join(state, lax.dynamic_index_in_dim(gathered, turn, 0, False).astype(x.dtype))

    return lax.fori_loop(0, place, one, state)


def normalize(frame_block):
    feat_width = frame_block.shape[-1]
    flat_rows = frame_block.reshape(-1, feat_width).astype(jnp.float32)
    normed = flat_rows * lax.rsqrt(jnp.mean(flat_rows * flat_rows, axis=-1, keepdims=True) + 1e-06)
    return normed.astype(jnp.bfloat16).reshape(frame_block.shape)


def project(normed, weights):
    head_count = weights.shape[1]
    head_size = weights.shape[2]
    normed = normed.reshape(-1, head_count, head_size)
    mapped = jnp.einsum("thd,khde->kthe", normed, weights, preferred_element_type=jnp.float32)
    queries = jax.nn.relu(mapped[0]).astype(jnp.bfloat16)
    key_rows = jax.nn.relu(mapped[1]).astype(jnp.bfloat16)
    value_rows = mapped[2].astype(jnp.bfloat16)
    gating = jax.nn.sigmoid(mapped[3])
    return (queries, key_rows, value_rows, gating)


def local_state(key_rows, value_rows):
    return jnp.einsum("thd,the->hde", key_rows, value_rows, preferred_element_type=jnp.float32)


def attend(queries, state):
    return jnp.einsum(
        "thd,hde->the", queries.astype(jnp.float32), state, precision=lax.Precision.HIGHEST
    )


def finish(frame_block, gating, attended):
    inv_rms = lax.rsqrt(jnp.mean(attended * attended, axis=-1, keepdims=True) + 1e-05)
    branch = (gating * attended * inv_rms).reshape(frame_block.shape)
    return (frame_block.astype(jnp.float32) + branch).astype(jnp.bfloat16)


def add_states(earlier, later):
    return earlier + later


def body(latents, spatial_weights, causal_weights):
    queries, key_rows, value_rows, gating = project(normalize(latents), spatial_weights)
    frame_state = lax.psum(local_state(key_rows, value_rows), "row")
    mixed_video = finish(latents, gating, attend(queries, frame_state))
    normed_c = normalize(mixed_video)
    mixed_heads, normed_heads = (
        lax.all_to_all(mixed_video, "row", split_axis=3, concat_axis=1, tiled=True),
        lax.all_to_all(normed_c, "row", split_axis=3, concat_axis=1, tiled=True),
    )
    head_part = causal_weights.shape[1] // lax.axis_size("row")
    head_start = lax.axis_index("row") * head_part
    local_weights = lax.dynamic_slice_in_dim(causal_weights, head_start, head_part, 1)
    queries, key_rows, value_rows, gating = project(normed_heads, local_weights)
    own_state = local_state(key_rows, value_rows)
    flat_state = own_state.reshape(-1, 128)
    earlier_flat = prefix(flat_state, "frame", add_states, jnp.zeros_like(flat_state))
    earlier = earlier_flat.reshape(own_state.shape)
    attended = attend(queries, earlier + own_state)
    return finish(mixed_heads, gating, attended)


def solution(mesh):
    in_specs = (P(("group", "frame"), "row", None, None), P(), P())
    out_specs = P(("group", "frame"), None, None, "row")
    return jax.shard_map(body, mesh=mesh, in_specs=in_specs, out_specs=out_specs, check_vma=False)
```

profile of v0, /device:TPU:27, one launch (start us, length us, event | category | flops | bytes accessed | tf_op | source)
XLA Modules:
  0.0 119.3 jit_solution(12640229504760504047)
XLA Ops:
  6.5 1.6 %reshape.152 = f32[128,10,112]{2,1,0:T(8,128)S(1)} reshape(bf16[1,4,32,1120]{3,2,1,0:T(8,128)(2,1)} %param.5) | data formatting | bytes 860160 | tf_op jit(solution)/shard_map/convert_element_type | solution.py:20
  8.2 1.1 multiply_reduce_fusion
  10.1 1.1 fusion.24
  11.3 20.5 %all-reduce.2.cloned.1.call-done = f32[10,112,112]{2,1,0:T(8,128)} async-done(((f32[10,112,112]{2,1,0:T(8,128)}), f32[10,112,112]{2,1,0:T(8,128)}) %all-reduce.2.cloned.1.call-update) | async-done | bytes 501776 | tf_op jit(solution)/shard_map/psum | solution.py:59
  31.8 1.7 %multiply_reduce_fusion.2 = (f32[128,10]{0,1:T(8,128)S(1)}, f32[128,10,112]{0,2,1:T(8,128)S(1)}) fusion(f32[10,112,112]{2,1,0:T(8,128)} %all-reduce.2.cloned.1.call-done, f32[4,128,10,112]{1,3,0,2:T(8,128)S(1)} %convolution_bitcast_fusion.1), kind=kOutput, calls=%fused_computation.40 | convolution fusion | flops 193391360 | bytes 1367040 | tf_op jit(solution)/shard_map/thd,hde->the/dot_general | solution.py:42
  33.5 1.0 fusion.18
  34.5 1.6 %copy.24 = f32[128,10,112]{2,1,0:T(8,128)S(1)} copy(f32[128,10,112]{0,2,1:T(8,128)} %fusion.18) | data formatting | bytes 1146880 | tf_op jit(solution)/shard_map/mul | solution.py:49
  36.6 1.4 %copy.25 = bf16[1,4,32,1120]{2,1,0,3:T(4,128)(2,1)S(1)} copy(bf16[1,4,32,1120]{3,2,1,0:T(8,128)(2,1)S(1)} %get-tuple-element.38) | data formatting | bytes 573440 | tf_op jit(solution)/shard_map/convert_element_type | solution.py:50
  38.8 2.2 %copy.28 = bf16[1,4,32,1120]{2,1,0,3:T(4,128)(2,1)S(1)} copy(bf16[1,4,32,1120]{3,2,1,0:T(8,128)(2,1)} %fusion.2) | data formatting | bytes 573440 | tf_op jit(solution)/shard_map/convert_element_type | solution.py:22
  41.0 1.8 %reshape.159 = bf16[2,2,35840]{2,1,0:T(2,128)(2,1)} reshape(bf16[1120,1,4,32]{3,2,1,0:T(4,128)(2,1)S(1)} %bitcast.72) | data formatting | bytes 573440
  42.8 5.7 %all_to_all.24 = bf16[2,2,35840]{2,1,0:T(2,128)(2,1)} all-to-all(bf16[2,2,35840]{2,1,0:T(2,128)(2,1)} %reshape.159), channel_id=1, replica_groups=mesh['group'=2,'frame'=8,'row'=2] {'row'}, dimensions={0} | all-to-all | bytes 573440 | tf_op jit(solution)/shard_map/all_to_all | solution.py:64
  48.5 1.7 %reshape.160 = bf16[1120,1,4,32]{3,2,1,0:T(4,128)(2,1)S(1)} reshape(bf16[2,2,35840]{2,1,0:T(2,128)(2,1)} %all_to_all.24) | data formatting | bytes 573440
  50.2 1.4 %copy.29 = bf16[1,4,32,2,560]{4,2,1,3,0:T(8,128)(2,1)} copy(bf16[1,4,32,2,560]{2,1,4,3,0:T(4,128)(2,1)S(1)} %bitcast.73) | data formatting | bytes 573440 | tf_op jit(solution)/shard_map/all_to_all | solution.py:64
  51.5 1.4 %reshape.148 = bf16[256,5,112]{2,1,0:T(8,128)(2,1)S(1)} reshape(bf16[1,2,4,32,560]{4,3,2,1,0:T(8,128)(2,1)} %bitcast.76) | data formatting | bytes 573440 | tf_op jit(solution)/shard_map/reshape | solution.py:28
  52.9 1.6 %convolution_bitcast_fusion = f32[4,256,5,112]{1,3,0,2:T(8,128)S(1)} fusion(bf16[256,5,112,1]{2,1,0,3:T(8,128)(2,1)S(1)} %bitcast.75, bf16[4,10,112,112]{3,2,1,0:T(8,128)(2,1)} %param.7, s32[]{:T(128)S(6)} %select_n.7), kind=kOutput, calls=%fused_computation.1 | convolution fusion | flops 128450560 | bytes 3153924 | tf_op jit(solution)/shard_map/thd,khde->kthe/dot_general | solution.py:29
  54.5 1.4 %copy-done.1 = f32[4,256,5,112]{1,3,0,2:T(8,128)} copy-done((f32[4,256,5,112]{1,3,0,2:T(8,128)}, f32[4,256,5,112]{1,3,0,2:T(8,128)S(1)}, u32[]{:S(2)}) %copy-start.1) | copy-done | bytes 2293784
  56.4 28.5 %all_gather.4 = bf16[8,490,128]{2,1,0:T(8,128)(2,1)} all-gather(bf16[1,490,128]{2,1,0:T(8,128)(2,1)S(1)} %convert_element_type.131), channel_id=1, replica_groups=mesh['group'=2,'frame'=8,'row'=2] {'frame'}, dimensions={0}, use_global_device_ids=true | all-gather | bytes 1128960 | tf_op jit(solution)/shard_map/all_gather | solution.py:9
  84.9 6.8 %while.10 = (s32[]{:T(128)}, f32[490,128]{1,0:T(8,128)S(1)}, s32[]{:T(128)}, bf16[8,490,128]{2,1,0:T(8,128)(2,1)}, s32[]{:T(128)}, /*index=5*/s32[]{:T(128)}, s32[]{:T(128)}) while((s32[]{:T(128)}, f32[490,128]{1,0:T(8,128)S(1)}, s32[]{:T(128)}, bf16[8,490,128]{2,1,0:T(8,128)(2,1)}, s32[]{:T(128)}, /*index=5*/s32[]{:T(128)}, s32[]{:T(128)}) %tuple.22), condition=%wide.region_5.6_spmd, body=%wide.region_4.5_spmd.sunk | while | flops 125445 | bytes 627315 | solution.py:15
  85.0 0.9 convert_add_fusion.2
  85.9 0.9 convert_add_fusion.2
  86.9 0.9 convert_add_fusion.2
  87.9 0.9 convert_add_fusion.2
  88.8 0.9 convert_add_fusion.2
  89.8 0.9 convert_add_fusion.2
  90.8 0.9 convert_add_fusion.2
  91.9 1.5 %multiply_reduce_fusion.1 = (f32[256,5]{0,1:T(8,128)S(1)}, f32[256,5,112]{0,2,1:T(8,128)S(1)}) fusion(f32[4,256,5,112]{1,3,0,2:T(8,128)} %copy-done.1, f32[5,112,112]{2,1,0:T(8,128)S(1)} %reshape.149, f32[5,112,112]{2,1,0:T(8,128)S(1)} %get-tuple-element.42), kind=kOutput, calls=%fused_computation.39 | convolution fusion | flops 193454080 | bytes 1367040 | tf_op jit(solution)/shard_map/thd,hde->the/dot_general | solution.py:42
  93.5 2.0 %fusion.10 = f32[256,5,112]{0,2,1:T(8,128)} fusion(f32[256,5,112]{0,2,1:T(8,128)S(1)} %get-tuple-element.44, f32[4,256,5,112]{1,3,0,2:T(8,128)} %copy-done.1, f32[256,5]{0,1:T(8,128)S(1)} %add_rsqrt_fusion), kind=kLoop, calls=%fused_computation.25 | loop fusion | flops 716800 | bytes 1725440 | tf_op jit(solution)/shard_map/mul | solution.py:49
  95.5 1.5 %copy.32 = f32[256,5,112]{2,1,0:T(8,128)S(1)} copy(f32[256,5,112]{0,2,1:T(8,128)} %fusion.10) | data formatting | bytes 1146880 | tf_op jit(solution)/shard_map/mul | solution.py:49
  97.0 1.1 reshape.150
  98.0 1.1 reshape.157
  99.2 10.2 %all_to_all.25 = bf16[2,2,35840]{2,1,0:T(2,128)(2,1)S(1)} all-to-all(bf16[2,2,35840]{2,1,0:T(2,128)(2,1)S(1)} %reshape.157), channel_id=1, replica_groups=mesh['group'=2,'frame'=8,'row'=2] {'row'}, dimensions={0} | all-to-all | bytes 573440 | tf_op jit(solution)/shard_map/all_to_all | solution.py:63
  110.6 1.9 %add_convert_fusion = bf16[1,8,32,560]{3,2,1,0:T(8,128)(2,1)} fusion(f32[1,8,32,560]{3,2,1,0:T(8,128)S(1)} %bitcast.74, f32[1,8,32,560]{3,2,1,0:T(8,128)} %reshape.150), kind=kLoop, calls=%fused_computation.9 | loop fusion | flops 286720 | bytes 1433600 | tf_op jit(solution)/shard_map/convert_element_type | solution.py:50
  (23 shorter events, 4.1 us)
Async XLA Ops:
  6.5 3.1 %copy-start = (bf16[4,10,112,112]{3,2,1,0:T(8,128)(2,1)S(1)}, bf16[4,10,112,112]{3,2,1,0:T(8,128)(2,1)}, u32[]{:S(2)}) copy-start(bf16[4,10,112,112]{3,2,1,0:T(8,128)(2,1)} %param.6) | copy-start | bytes 3010564
  6.5 25.2 %all-reduce.2.cloned.1.call-start = ((), (), s32[]{:S(2)}) async-start(), calls=%async_computation.2 | async-start | bytes 1146880 | tf_op jit(solution)/shard_map/psum | solution.py:59
  34.5 1.9 %copy-start.2 = (bf16[1,4,32,1120]{3,2,1,0:T(8,128)(2,1)S(1)}, bf16[1,4,32,1120]{3,2,1,0:T(8,128)(2,1)}, u32[]{:S(2)}) copy-start(bf16[1,4,32,1120]{3,2,1,0:T(8,128)(2,1)} %param.5) | copy-start | bytes 860164
  54.5 1.4 %copy-start.1 = (f32[4,256,5,112]{1,3,0,2:T(8,128)}, f32[4,256,5,112]{1,3,0,2:T(8,128)S(1)}, u32[]{:S(2)}) copy-start(f32[4,256,5,112]{1,3,0,2:T(8,128)S(1)} %convolution_bitcast_fusion) | copy-start | bytes 6881284
Sparse Core Ops, SparseCore 0:
  11.4 20.3 all-reduce.1
where the time goes:
time: 120 us; the launch traced here: 119 us
  blocking collectives  44.3 us (37%)
  waiting for transfers between devices  20.5 us (17%)
  local copies, waits for them, and re-layouts  20.1 us (17%)
  other arithmetic  13.8 us (12%)
  between operations  13.6 us (11%)
  matrix products  6.67 us (6%)
    all_gather x1, blocking collectives, prefix(): gathered = lax.all_gather(x.astype(jnp.bfloat16), axis)  28.5 us
    psum x1, waiting for transfers between devices, body(): frame_state = lax.psum(local_state(key_rows, value_rows), 'row')  20.5 us
    all_to_all x1, blocking collectives, body(): lax.all_to_all(mixed_video, 'row', split_axis=3, concat_axis=1, tiled=True)  10.2 us
    add x7, other arithmetic, add_states(): return earlier + later  6.6 us
    unnamed x10, local copies, waits for them, and re-layouts  6.55 us
    all_to_all x1, blocking collectives, body(): lax.all_to_all(normed_c, 'row', split_axis=3, concat_axis=1, tiled=True)  5.67 us
    dot_general x2, matrix products, attend(): jnp.einsum('thd,hde->the', queries.astype(jnp.float32), state, precision=...  3.21 us
    mul x2, local copies, waits for them, and re-layouts, finish(): branch = (gating * attended * inv_rms).reshape(frame_block.shape)  3.07 us
  transfers between devices with their start and end apart: 1, of which 1 were waited for; matrix products, arithmetic and copies ran while one was open for 0% of the time, Pallas kernels for 0%

commit v1 on v0

--- a/solution.py
+++ b/solution.py
@@ -2,6 +2,11 @@
 import jax.numpy as jnp
 from jax import lax
 from jax.sharding import PartitionSpec as P
+
+
+def column_wrap(local):
+    main = jnp.sum(jax.lax.all_gather(local, axis_name="row"), axis=0)
+    return main
 
 
 def prefix(x, axis, join, neutral):
@@ -56,7 +61,7 @@
 
 def body(latents, spatial_weights, causal_weights):
     queries, key_rows, value_rows, gating = project(normalize(latents), spatial_weights)
-    frame_state = lax.psum(local_state(key_rows, value_rows), "row")
+    frame_state = column_wrap(local_state(key_rows, value_rows))
     mixed_video = finish(latents, gating, attend(queries, frame_state))
     normed_c = normalize(mixed_video)
     mixed_heads, normed_heads = (

time: 120 us -> 75.4 us (0.63)
  the two profiles are of different devices: /device:TPU:27 before, /device:TPU:0 now
where the time goes in v1:
time: 75.4 us; the launch traced here: 74.8 us
  blocking collectives  37.6 us (50%)
  local copies, waits for them, and re-layouts  16.3 us (22%)
  other arithmetic  7.94 us (11%)
  starting transfers between devices  6.9 us (9%)
  matrix products  5.85 us (8%)
    all_gather x1, blocking collectives, prefix(): gathered = lax.all_gather(x.astype(jnp.bfloat16), axis)  34.7 us
    unnamed x10, local copies, waits for them, and re-layouts  6.14 us
    all_to_all x1, starting transfers between devices, body(): lax.all_to_all(mixed_video, 'row', split_axis=3, concat_axis=1, tiled=True)  3.45 us
    all_to_all x1, starting transfers between devices, body(): lax.all_to_all(normed_c, 'row', split_axis=3, concat_axis=1, tiled=True)  3.45 us
    dot_general x2, matrix products, attend(): jnp.einsum('thd,hde->the', queries.astype(jnp.float32), state, precision=...  3.21 us
    all_gather x1, blocking collectives, column_wrap(): main = jnp.sum(jax.lax.all_gather(local, axis_name='row'), axis=0)  2.87 us
    reduce_sum x1, other arithmetic, column_wrap(): main = jnp.sum(jax.lax.all_gather(local, axis_name='row'), axis=0)  2.23 us
    mul x2, other arithmetic, finish(): branch = (gating * attended * inv_rms).reshape(frame_block.shape)  2.19 us
  transfers between devices with their start and end apart: 2, of which 0 were waited for; matrix products, arithmetic and copies ran while one was open for 15% of the time, Pallas kernels for 0%

profile of v1, /device:TPU:0, one launch (start us, length us, event | category | flops | bytes accessed | tf_op | source)
XLA Modules:
  0.0 74.8 jit_solution(14493470499125631938)
XLA Ops:
  0.0 1.6 %reshape.152 = f32[128,10,112]{2,1,0:T(8,128)S(1)} reshape(bf16[1,4,32,1120]{3,2,1,0:T(8,128)(2,1)} %param.5) | data formatting | bytes 860160 | tf_op jit(solution)/shard_map/convert_element_type | solution.py:25
  1.6 1.1 %multiply_reduce_fusion = f32[4,32]{1,0:T(4,128)S(1)} fusion(bf16[1,4,32,1120]{3,2,1,0:T(8,128)(2,1)} %param.5), kind=kLoop, calls=%fused_computation.13 | loop fusion | flops 429952 | bytes 287232 | tf_op jit(solution)/shard_map/reduce_sum | solution.py:26
  2.8 0.2 fusion.20
  3.1 0.5 convolution_bitcast_fusion.1
  3.6 0.3 fusion.24
  3.9 2.9 %all-gather = f32[20,112,112]{2,1,0:T(8,128)} all-gather(f32[10,112,112]{2,1,0:T(8,128)S(1)} %fusion.24), channel_id=2, replica_groups=mesh['group'=2,'frame'=8,'row'=2] {'row'}, dimensions={0}, use_global_device_ids=true | all-gather | bytes 1505280 | tf_op jit(solution)/shard_map/all_gather | solution.py:8
  6.8 2.2 %reduce_sum.46 = f32[10,112,112]{2,1,0:T(8,128)} reduce(f32[2,10,112,112]{3,2,1,0:T(8,128)} %bitcast.72, f32[]{:T(128)} %constant.18.clone.1), dimensions={0}, to_apply=%region_1.2 | reduce | flops 125440 | bytes 1505284 | tf_op jit(solution)/shard_map/reduce_sum | solution.py:8
  9.0 1.7 %multiply_reduce_fusion.2 = (f32[128,10]{0,1:T(8,128)S(1)}, f32[128,10,112]{0,2,1:T(8,128)S(1)}) fusion(f32[10,112,112]{2,1,0:T(8,128)} %reduce_sum.46, f32[4,128,10,112]{1,3,0,2:T(8,128)S(1)} %convolution_bitcast_fusion.1), kind=kOutput, calls=%fused_computation.40 | convolution fusion | flops 193391360 | bytes 1367040 | tf_op jit(solution)/shard_map/thd,hde->the/dot_general | solution.py:47
  10.7 1.0 %fusion.18 = f32[128,10,112]{0,2,1:T(8,128)} fusion(f32[128,10,112]{0,2,1:T(8,128)S(1)} %get-tuple-element.40, f32[4,128,10,112]{1,3,0,2:T(8,128)S(1)} %convolution_bitcast_fusion.1, f32[128,10]{0,1:T(8,128)S(1)} %add_rsqrt_fusion.1), kind=kLoop, calls=%fused_computation.37 | loop fusion | flops 716800 | bytes 1725440 | tf_op jit(solution)/shard_map/mul | solution.py:54
  11.7 1.6 %copy.24 = f32[128,10,112]{2,1,0:T(8,128)S(1)} copy(f32[128,10,112]{0,2,1:T(8,128)} %fusion.18) | data formatting | bytes 1146880 | tf_op jit(solution)/shard_map/mul | solution.py:54
  13.3 0.3 reshape.147
  13.9 1.4 %copy.28 = bf16[1,4,32,1120]{2,1,0,3:T(4,128)(2,1)S(1)} copy(bf16[1,4,32,1120]{3,2,1,0:T(8,128)(2,1)S(1)} %fusion.2) | data formatting | bytes 573440 | tf_op jit(solution)/shard_map/convert_element_type | solution.py:27
  15.3 1.8 %reshape.160 = bf16[2,2,35840]{2,1,0:T(2,128)(2,1)} reshape(bf16[1120,1,4,32]{3,2,1,0:T(4,128)(2,1)S(1)} %bitcast.73) | data formatting | bytes 573440
  17.1 3.4 %all-to-all-start.1 = ((bf16[2,2,35840]{2,1,0:T(2,128)(2,1)}), bf16[2,2,35840]{2,1,0:T(2,128)(2,1)S(1)}, u32[]{:S(2)}, u32[]{:S(2)}) async-start(bf16[2,2,35840]{2,1,0:T(2,128)(2,1)} %reshape.160), calls=%async_computation.1 | async-start | bytes 573440 | tf_op jit(solution)/shard_map/all_to_all | solution.py:69
  20.6 1.4 %copy.25 = bf16[1,4,32,1120]{2,1,0,3:T(4,128)(2,1)S(1)} copy(bf16[1,4,32,1120]{3,2,1,0:T(8,128)(2,1)S(1)} %get-tuple-element.38) | data formatting | bytes 573440 | tf_op jit(solution)/shard_map/convert_element_type | solution.py:55
  22.0 1.8 %reshape.158 = bf16[2,2,35840]{2,1,0:T(2,128)(2,1)} reshape(bf16[1120,1,4,32]{3,2,1,0:T(4,128)(2,1)S(1)} %bitcast.74) | data formatting | bytes 573440
  23.8 3.4 %all-to-all-start = ((bf16[2,2,35840]{2,1,0:T(2,128)(2,1)}), bf16[2,2,35840]{2,1,0:T(2,128)(2,1)S(1)}, u32[]{:S(2)}, u32[]{:S(2)}) async-start(bf16[2,2,35840]{2,1,0:T(2,128)(2,1)} %reshape.158), calls=%async_computation | async-start | bytes 573440 | tf_op jit(solution)/shard_map/all_to_all | solution.py:68
  27.3 0.6 reshape.161
  27.9 0.7 copy.29
  28.6 0.4 reshape.148
  29.0 1.6 %convolution_bitcast_fusion = f32[4,256,5,112]{1,3,0,2:T(8,128)S(1)} fusion(bf16[256,5,112,1]{2,1,0,3:T(8,128)(2,1)S(1)} %bitcast.77, bf16[4,10,112,112]{3,2,1,0:T(8,128)(2,1)} %param.7, s32[]{:T(128)S(6)} %select_n.7), kind=kOutput, calls=%fused_computation.1 | convolution fusion | flops 128450560 | bytes 3153924 | tf_op jit(solution)/shard_map/thd,khde->kthe/dot_general | solution.py:34
  30.6 1.4 %copy-done.1 = f32[4,256,5,112]{1,3,0,2:T(8,128)} copy-done((f32[4,256,5,112]{1,3,0,2:T(8,128)}, f32[4,256,5,112]{1,3,0,2:T(8,128)S(1)}, u32[]{:S(2)}) %copy-start.1) | copy-done | bytes 2293784
  32.0 0.2 fusion.46
  32.2 0.3 convert_element_type.131
  32.5 34.7 %all_gather.12 = bf16[8,490,128]{2,1,0:T(8,128)(2,1)S(1)} all-gather(bf16[1,490,128]{2,1,0:T(8,128)(2,1)S(1)} %convert_element_type.131), channel_id=1, replica_groups=mesh['group'=2,'frame'=8,'row'=2] {'frame'}, dimensions={0}, use_global_device_ids=true | all-gather | bytes 1128960 | tf_op jit(solution)/shard_map/all_gather | solution.py:14
  67.4 1.5 %multiply_reduce_fusion.1 = (f32[256,5]{0,1:T(8,128)S(1)}, f32[256,5,112]{0,2,1:T(8,128)S(1)}) fusion(f32[4,256,5,112]{1,3,0,2:T(8,128)} %copy-done.1, f32[5,112,112]{2,1,0:T(8,128)S(1)} %reshape.149, f32[5,112,112]{2,1,0:T(8,128)S(1)} %get-tuple-element.42), kind=kOutput, calls=%fused_computation.39 | convolution fusion | flops 193454080 | bytes 1367040 | tf_op jit(solution)/shard_map/thd,hde->the/dot_general | solution.py:47
  68.9 1.2 %fusion.10 = f32[256,5,112]{0,2,1:T(8,128)S(1)} fusion(f32[256,5,112]{0,2,1:T(8,128)S(1)} %get-tuple-element.44, f32[4,256,5,112]{1,3,0,2:T(8,128)} %copy-done.1, f32[256,5]{0,1:T(8,128)S(1)} %add_rsqrt_fusion), kind=kLoop, calls=%fused_computation.25 | loop fusion | flops 716800 | bytes 1725440 | tf_op jit(solution)/shard_map/mul | solution.py:54
  70.2 0.4 copy.32
  70.6 1.1 %reshape.150 = f32[1,8,32,560]{3,2,1,0:T(8,128)} reshape(f32[256,5,112]{2,1,0:T(8,128)S(1)} %copy.32) | data formatting | bytes 1146880 | tf_op jit(solution)/shard_map/reshape | solution.py:54
  71.6 0.6 reshape.159
  72.2 0.7 copy.26
  72.9 1.9 %add_convert_fusion = bf16[1,8,32,560]{3,2,1,0:T(8,128)(2,1)} fusion(f32[1,8,32,560]{3,2,1,0:T(8,128)S(1)} %bitcast.76, f32[1,8,32,560]{3,2,1,0:T(8,128)} %reshape.150), kind=kLoop, calls=%fused_computation.9 | loop fusion | flops 286720 | bytes 1433600 | tf_op jit(solution)/shard_map/convert_element_type | solution.py:55
  (17 shorter events, 0.6 us)
Async XLA Ops:
  0.0 3.1 %copy-start = (bf16[4,10,112,112]{3,2,1,0:T(8,128)(2,1)S(1)}, bf16[4,10,112,112]{3,2,1,0:T(8,128)(2,1)}, u32[]{:S(2)}) copy-start(bf16[4,10,112,112]{3,2,1,0:T(8,128)(2,1)} %param.6) | copy-start | bytes 3010564
  11.7 1.9 %copy-start.2 = (bf16[1,4,32,1120]{3,2,1,0:T(8,128)(2,1)S(1)}, bf16[1,4,32,1120]{3,2,1,0:T(8,128)(2,1)}, u32[]{:S(2)}) copy-start(bf16[1,4,32,1120]{3,2,1,0:T(8,128)(2,1)} %param.5) | copy-start | bytes 860164
  17.1 6.7 %all-to-all-start.1 = ((bf16[2,2,35840]{2,1,0:T(2,128)(2,1)}), bf16[2,2,35840]{2,1,0:T(2,128)(2,1)S(1)}, u32[]{:S(2)}, u32[]{:S(2)}) async-start(bf16[2,2,35840]{2,1,0:T(2,128)(2,1)} %reshape.160), calls=%async_computation.1 | async-start | bytes 573440 | tf_op jit(solution)/shard_map/all_to_all | solution.py:69
  23.8 47.8 %all-to-all-start = ((bf16[2,2,35840]{2,1,0:T(2,128)(2,1)}), bf16[2,2,35840]{2,1,0:T(2,128)(2,1)S(1)}, u32[]{:S(2)}, u32[]{:S(2)}) async-start(bf16[2,2,35840]{2,1,0:T(2,128)(2,1)} %reshape.158), calls=%async_computation | async-start | bytes 573440 | tf_op jit(solution)/shard_map/all_to_all | solution.py:68
  30.6 1.4 %copy-start.1 = (f32[4,256,5,112]{1,3,0,2:T(8,128)}, f32[4,256,5,112]{1,3,0,2:T(8,128)S(1)}, u32[]{:S(2)}) copy-start(f32[4,256,5,112]{1,3,0,2:T(8,128)S(1)} %convolution_bitcast_fusion) | copy-start | bytes 6881284
